TPU v7x, 512 devices: a whole 4x8x8 slice. The times are simulated.
512 devices in a mesh: region: 32 (over x, z), batch: 16 (over y, core).
Axes of the slice: x: 4, y: 8, z: 8, core: 2. Of those that a mesh axis runs over, the one named last changes fastest.
Arguments:
- basis_values: bfloat16 [128, 2, 4096, 512], P('region', None, 'batch'), may hold values from -6 to 6
- dens_tiles: bfloat16 [128, 512, 512], P('region', 'batch'), may hold values from -0.005859375 to 0.005859375
- region_tiles: int32 [128, 3], replicated, may hold values from 0 to 127, as said below
- point_counts: int32 [128, 16], P('region', 'batch'), may hold values from 64 to 256, as said below
- point_weights: float32 [128, 4096], P('region', 'batch'), may hold values from 0.0078125 to 0.03125
Outputs:
- xc_tiles: float32 [128, 512, 512], P('region', 'batch')
Inputs may be any that keep to these rules, and one draw needn't show every extreme that they name: `region_tiles`: tile t is stored on index t // 4 of region. Regions 4 * i to 4 * i + 3 lie on index i; among their 12 entries no owner index holds more than 1 and some owner holds exactly 1, on every index; the entries of one owner on one index are different tiles. `point_counts`: every region has at least one batch with all 256 points live.
All inputs are finite; a program needn't handle non-finite values.
Results may differ from a plain program's by a relative error of at most 0.004.
Values may be sent and summed in bfloat16 or wider, within the bound.
A program may use at most 64 MiB of HBM per device.

v0:
```python
import jax
import jax.numpy as jnp
from jax import lax
from jax.sharding import PartitionSpec as P

SLATER = 0.9847450218426964


def potential(density):
    return -SLATER * density * jnp.power(density * density + 1.0, -1.0 / 3.0)


def shards(basis_values, dens_tiles, region_tiles, point_counts, point_weights):
    owner_count = lax.axis_size("region")
    batch_count = lax.axis_size("batch")
    my_index = lax.axis_index("region")
    region_local = basis_values.shape[0]
    point_local = basis_values.shape[2]
    tile_local = dens_tiles.shape[0]
    row_count = dens_tiles.shape[1]
    block_width = dens_tiles.shape[2]
    requests = 3 * region_local
    slot_total = (requests + owner_count - 1) // owner_count
    table = region_tiles.reshape(owner_count, requests)
    owners = table // tile_local
    local_ids = table % tile_local
    order = jnp.arange(requests, dtype=jnp.int32)
    earlier = (owners[:, :, None] == owners[:, None, :]) & (
        order[None, None, :] < order[None, :, None]
    )
    ranks = jnp.sum(earlier.astype(jnp.int32), axis=2)
    slot_ids = jnp.arange(slot_total, dtype=jnp.int32)
    tile_ids = jnp.arange(tile_local, dtype=jnp.int32)
    chosen = (
        (owners == my_index)[:, :, None, None]
        & (ranks[:, :, None, None] == slot_ids[None, None, :, None])
        & (local_ids[:, :, None, None] == tile_ids[None, None, None, :])
    )
    selector = jnp.sum(chosen.astype(jnp.float32), axis=1)
    my_owners = lax.dynamic_index_in_dim(owners, my_index, 0, keepdims=False)
    my_ranks = lax.dynamic_index_in_dim(ranks, my_index, 0, keepdims=False)
    outgoing = jnp.einsum(
        "dct,trb->dcrb",
        selector.astype(jnp.bfloat16),
        dens_tiles,
        preferred_element_type=jnp.float32,
    ).astype(jnp.bfloat16)
    incoming = lax.all_to_all(outgoing, "region", split_axis=0, concat_axis=0, tiled=True)
    flat = incoming.reshape(owner_count * slot_total, row_count, block_width)
    fetched = jnp.take(flat, my_owners * slot_total + my_ranks, axis=0)
    piece = lax.all_gather(fetched, "batch", axis=1, tiled=True)
    count = piece.shape[1]
    shaped = piece.reshape(region_local, 3, count, block_width)
    left_aa = jnp.einsum(
        "rpc,rcb->rpb", basis_values[:, 0], shaped[:, 0], preferred_element_type=jnp.float32
    )
    left_ab = jnp.einsum(
        "rpc,rcb->rpb", basis_values[:, 0], shaped[:, 1], preferred_element_type=jnp.float32
    )
    left_bb = jnp.einsum(
        "rpc,rcb->rpb", basis_values[:, 1], shaped[:, 2], preferred_element_type=jnp.float32
    )
    left_aa, left_ab, left_bb = (left_aa, left_ab, left_bb)
    phi_a = basis_values[:, 0]
    phi_b = basis_values[:, 1]
    density = (
        jnp.sum(phi_a * left_aa, axis=-1)
        + 2.0 * jnp.sum(phi_b * left_ab, axis=-1)
        + jnp.sum(phi_b * left_bb, axis=-1)
    )
    live = jnp.arange(point_local, dtype=jnp.int32)[None, :] < point_counts
    scale = jnp.where(live, point_weights * potential(density), 0.0)
    scaled_a = (scale[:, :, None] * phi_a).astype(jnp.bfloat16)
    scaled_b = (scale[:, :, None] * phi_b).astype(jnp.bfloat16)
    first = jnp.einsum("rpc,rpb->crb", phi_a, scaled_a, preferred_element_type=jnp.float32)
    second = jnp.einsum("rpc,rpb->crb", phi_a, scaled_b, preferred_element_type=jnp.float32)
    third = jnp.einsum("rpc,rpb->crb", phi_b, scaled_b, preferred_element_type=jnp.float32)
    partial_pairs = jnp.stack([first, second, third], axis=2).reshape(
        block_width, requests, block_width
    )
    partial_pairs = partial_pairs.astype(jnp.bfloat16).reshape(
        batch_count, row_count, requests, block_width
    )
    received = lax.all_to_all(partial_pairs, "batch", split_axis=0, concat_axis=0, tiled=True)
    pairs = jnp.sum(received.astype(jnp.float32), axis=0)
    placement = (
        (my_owners[:, None, None] == jnp.arange(owner_count, dtype=jnp.int32)[None, :, None])
        & (my_ranks[:, None, None] == slot_ids[None, None, :])
    ).astype(jnp.float32)
    outgoing_sums = jnp.einsum("jdc,rjb->dcrb", placement, pairs, precision=lax.Precision.HIGHEST)
    returned = lax.all_to_all(outgoing_sums, "region", split_axis=0, concat_axis=0, tiled=True)
    return jnp.einsum("dct,dcrb->trb", selector, returned, precision=lax.Precision.HIGHEST)


def solution(mesh):
    return jax.shard_map(
        shards,
        mesh=mesh,
        in_specs=(
            P("region", None, "batch", None),
            P("region", "batch", None),
            P(),
            P("region", "batch"),
            P("region", "batch"),
        ),
        out_specs=P("region", "batch", None),
        check_vma=False,
    )
```

profile of v0, /device:TPU:1, one launch (start us, length us, event | category | flops | bytes accessed | tf_op | source)
XLA Modules:
  0.0 331.1 jit_solution(2894611914320594194)
XLA Ops:
  6.5 0.8 copy.81
  7.4 0.1 reshape.254
  7.4 0.1 copy.82
  7.6 0.1 convert_reduce_fusion.1
  7.7 0.5 fusion.14
  8.2 1.6 copy.88
  9.8 13.8 %all-to-all-start = ((bf16[32,1,32,512]{3,2,1,0:T(8,128)(2,1)}), bf16[32,1,32,512]{3,2,1,0:T(8,128)(2,1)S(1)}, u32[]{:S(2)}, u32[]{:S(2)}) async-start(bf16[32,1,32,512]{3,2,1,0:T(8,128)(2,1)} %copy.88), calls=%async_computation | async-start | bytes 2097152 | tf_op jit(solution)/shard_map/all_to_all | solution.py:48
  23.6 0.0 all-gather.2.cloned.1.call-start
  23.7 0.2 dynamic-slice_reduce_fusion
  24.0 24.3 %all-to-all-done = bf16[32,1,32,512]{3,2,1,0:T(8,128)(2,1)S(1)} async-done(((bf16[32,1,32,512]{3,2,1,0:T(8,128)(2,1)}), bf16[32,1,32,512]{3,2,1,0:T(8,128)(2,1)S(1)}, u32[]{:S(2)}, u32[]{:S(2)}) %all-to-all-start) | async-done | bytes 1048608 | tf_op jit(solution)/shard_map/all_to_all | solution.py:48
  48.3 1.4 gather_fusion
  49.6 1.9 broadcast_select_fusion
  51.5 0.0 all-gather.2.cloned.1.call-update
  51.5 49.9 %all-gather.2.cloned.1.call-done = bf16[12,512,512]{2,1,0:T(8,128)(2,1)} async-done(((bf16[12,32,512]{2,1,0:T(8,128)(2,1)}), bf16[12,512,512]{2,1,0:T(8,128)(2,1)}) %all-gather.2.cloned.1.call-update) | async-done | bytes 6291472 | tf_op jit(solution)/shard_map/all_gather | solution.py:51
  101.5 2.5 fusion.2
  104.0 0.9 copy-done.4
  104.9 0.8 fusion
  105.7 0.8 fusion.3
  106.5 0.1 multiply_select_fusion
  106.6 0.9 convert_bitcast_fusion.1
  107.5 0.9 convert_bitcast_fusion
  108.4 0.9 convert_bitcast_fusion.2
  109.4 0.8 pad_maximum_fusion
  110.2 0.4 copy.99
  110.6 1.1 copy.100
  111.8 145.4 %all_to_all.15 = bf16[16,32,12,512]{3,1,2,0:T(8,128)(2,1)S(1)} all-to-all(bf16[16,32,12,512]{3,1,2,0:T(8,128)(2,1)S(1)} %copy.100), channel_id=1, replica_groups=mesh['region'=32,'batch'=16] {'batch'}, dimensions={0} | all-to-all | bytes 12582912 | tf_op jit(solution)/shard_map/all_to_all | solution.py:84
  257.1 1.3 convert_reduce_fusion
  258.4 1.4 convolution_bitcast_fusion
  259.8 1.2 copy.103
  261.0 60.3 %all_to_all.16 = f32[32,1,32,512]{3,2,1,0:T(8,128)S(1)} all-to-all(f32[32,1,32,512]{3,2,1,0:T(8,128)S(1)} %copy.103), channel_id=1, replica_groups=mesh['region'=32,'batch'=16] {'region'}, dimensions={0} | all-to-all | bytes 4194304 | tf_op jit(solution)/shard_map/all_to_all | solution.py:91
  321.3 2.2 fusion.8
  323.5 0.8 copy.105
  (16 shorter events, 0.1 us)
Async XLA Ops:
  6.5 1.2 copy-start
  9.8 91.7 %copy-start.1 = (bf16[4,2,256,512]{3,2,1,0:T(8,128)(2,1)S(1)}, bf16[4,2,256,512]{3,2,1,0:T(8,128)(2,1)}, u32[]{:S(2)}) copy-start(bf16[4,2,256,512]{3,2,1,0:T(8,128)(2,1)} %param.5) | copy-start | bytes 6291460
  9.8 38.5 %all-to-all-start = ((bf16[32,1,32,512]{3,2,1,0:T(8,128)(2,1)}), bf16[32,1,32,512]{3,2,1,0:T(8,128)(2,1)S(1)}, u32[]{:S(2)}, u32[]{:S(2)}) async-start(bf16[32,1,32,512]{3,2,1,0:T(8,128)(2,1)} %copy.88), calls=%async_computation | async-start | bytes 2097152 | tf_op jit(solution)/shard_map/all_to_all | solution.py:48
  23.6 77.8 %all-gather.2.cloned.1.call-start = ((), (), s32[]{:S(2)}) async-start(), calls=%async_computation.3 | async-start | bytes 6684672 | tf_op jit(solution)/shard_map/all_gather | solution.py:51
  101.5 3.4 %copy-start.4 = (bf16[12,512,512]{2,1,0:T(8,128)(2,1)S(1)}, bf16[12,512,512]{2,1,0:T(8,128)(2,1)}, u32[]{:S(2)}) copy-start(bf16[12,512,512]{2,1,0:T(8,128)(2,1)} %all-gather.2.cloned.1.call-done) | copy-start | bytes 18874372
  105.7 0.8 copy-start.2
  105.7 0.8 copy-start.3
Sparse Core Ops, SparseCore 0:
  51.6 49.7 all-gather.1
where the time goes:
time: 331 us
  blocking collectives  206 us (62%)
  waiting for transfers between devices  74.3 us (22%)
  starting transfers between devices  13.9 us (4%)
  between operations  13.6 us (4%)
  matrix products  11 us (3%)
  local copies, waits for them, and re-layouts  8.33 us (3%)
  other arithmetic  4.43 us (1%)
    all_to_all x1, blocking collectives, shards(): lax.all_to_all(partial_pairs, 'batch', split_axis=0, concat_axis=0, tiled...  145 us
    all_to_all x1, blocking collectives, shards(): lax.all_to_all(outgoing_sums, 'region', split_axis=0, concat_axis=0, tile...  60.3 us
    all_gather x1, waiting for transfers between devices, shards(): piece = lax.all_gather(fetched, 'batch', axis=1, tiled=True)  49.9 us
    all_to_all x1, waiting for transfers between devices, shards(): lax.all_to_all(outgoing, 'region', split_axis=0, concat_axis=0, tiled=True)  24.3 us
    all_to_all x1, starting transfers between devices, shards(): lax.all_to_all(outgoing, 'region', split_axis=0, concat_axis=0, tiled=True)  13.8 us
  transfers between devices with their start and end apart: 2, of which 2 were waited for; matrix products, arithmetic and copies ran while one was open for 0% of the time, Pallas kernels for 0%

commit v1 on v0

v1 whole, which is shorter than its diff:
```python
import functools

import jax
import jax.numpy as jnp
from jax import lax
from jax.experimental import pallas as pl
from jax.experimental.pallas import tpu as pltpu
from jax.sharding import PartitionSpec as P

SLATER = 0.9847450218426964
MESH = pl.DeviceIdType.MESH


def potential(density):
    return -SLATER * density * jnp.exp(jnp.log(density * density + 1.0) * (-1.0 / 3.0))


def batch_kernel(
    ring, far, regions, rows, own_ref, phi_ref, weight_ref, out_ref,
    tiles, pairs, peer, sum_up, got_up, sum_down, got_down,
    up_send, up_recv, down_send, down_recv, side_send, side_recv,
    swap_send, swap_recv, red_up_send, red_up_recv, red_down_send, red_down_recv,
):
    near = ring - 1 - far
    me = lax.axis_index("batch")
    y, c = me // 2, me % 2
    way = 1 - 2 * c
    other = y * 2 + (1 - c)

    def at(k):
        return lax.rem(y + k * way + ring, ring)

    def mine(k):
        return at(k) * 2 + c

    def theirs(k):
        return at(k) * 2 + (1 - c)

    barrier = pltpu.get_barrier_semaphore()
    for target in (mine(1), mine(-1), other):
        pl.semaphore_signal(barrier, inc=1, device_id={"batch": target}, device_id_type=MESH)
    pl.semaphore_wait(barrier, 3)

    def remote(src, dst, send, recv, target):
        return pltpu.make_async_remote_copy(
            src_ref=src, dst_ref=dst, send_sem=send, recv_sem=recv,
            device_id={"batch": target}, device_id_type=MESH,
        )

    def part(r):
        return pl.ds(3 * r, 3)

    def block(r, slot):
        return tiles.at[part(r), slot]

    def up_hop(a, r):
        src = own_ref.at[part(r)] if a == 0 else block(r, mine(-a))
        return remote(src, block(r, mine(-a)), up_send.at[a, r], up_recv.at[a, r], mine(1))

    def up_arrival(a, r):
        slot = block(r, mine(-(a + 1)))
        return remote(slot, slot, up_send.at[a, r], up_recv.at[a, r], mine(1))

    def down_hop(a, r):
        src = own_ref.at[part(r)] if a == 0 else block(r, mine(a))
        return remote(src, block(r, mine(a)), down_send.at[a, r], down_recv.at[a, r], mine(-1))

    def down_arrival(a, r):
        slot = block(r, mine(a + 1))
        return remote(slot, slot, down_send.at[a, r], down_recv.at[a, r], mine(-1))

    def side(i, r):
        if i == 0:
            src, slot = own_ref.at[part(r)], block(r, me)
        else:
            slot = block(r, mine(-i if i <= far else i - far))
            src = slot
        return remote(src, slot, side_send.at[i, r], side_recv.at[i, r], other)

    def side_arrival(i, r):
        k = 0 if i == 0 else (i if i <= far else far - i)
        slot = block(r, theirs(k))
        return remote(slot, slot, side_send.at[i, r], side_recv.at[i, r], other)

    def gather_step(a, r):
        if a == 0:
            up_hop(0, r).start()
            down_hop(0, r).start()
            side(0, r).start()
            tiles[part(r), me] = own_ref[part(r)]
            return
        up_arrival(a - 1, r).wait_recv()
        if a < far:
            up_hop(a, r).start()
        side(a, r).start()
        if a <= near:
            down_arrival(a - 1, r).wait_recv()
            if a < near:
                down_hop(a, r).start()
            side(far + a, r).start()

    def swap(r):
        return remote(
            pairs.at[part(r), :, 1 - c], peer.at[part(r)],
            swap_send.at[r], swap_recv.at[r], other,
        )

    def compute(r):
        for i in range(ring):
            side_arrival(i, r).wait_recv()
        width = phi_ref.shape[-1]
        phi_a, phi_b = phi_ref[r, 0], phi_ref[r, 1]

        def left(values, j):
            matrix = tiles[3 * r + j].reshape(2 * ring * rows, width)
            return jnp.dot(values, matrix, preferred_element_type=jnp.float32)

        wide_a, wide_b = phi_a.astype(jnp.float32), phi_b.astype(jnp.float32)
        density = jnp.sum(
            wide_a * left(phi_a, 0) + wide_b * (2.0 * left(phi_a, 1) + left(phi_b, 2)),
            axis=1, keepdims=True,
        )
        scale = weight_ref[r] * potential(density)
        scaled_a = (scale * wide_a).astype(jnp.bfloat16)
        scaled_b = (scale * wide_b).astype(jnp.bfloat16)
        for j, (lhs, rhs) in enumerate(((phi_a, scaled_a), (phi_a, scaled_b), (phi_b, scaled_b))):
            product = lax.dot_general(
                lhs, rhs, (((0,), (0,)), ((), ())), preferred_element_type=jnp.float32
            )
            pairs[3 * r + j] = product.astype(jnp.bfloat16).reshape(ring, 2, rows, width)
        swap(r).start()

    def chip_sum(r, k):
        return pairs[part(r), at(k), c].astype(jnp.float32) + peer[part(r), at(k)].astype(jnp.float32)

    def red_up(s, r):
        return remote(
            sum_up.at[s, part(r)], got_up.at[s, part(r)],
            red_up_send.at[s, r], red_up_recv.at[s, r], mine(1),
        )

    def red_down(s, r):
        return remote(
            sum_down.at[s, part(r)], got_down.at[s, part(r)],
            red_down_send.at[s, r], red_down_recv.at[s, r], mine(-1),
        )

    def reduce_step(s, r):
        if s == 0:
            swap(r).wait_recv()
        total = chip_sum(r, far - s)
        if s > 0:
            red_up(s - 1, r).wait_recv()
            total = total + got_up[s - 1, part(r)].astype(jnp.float32)
        sum_up[s, part(r)] = total.astype(jnp.bfloat16)
        red_up(s, r).start()
        if s < near:
            total = chip_sum(r, s - near)
            if s > 0:
                red_down(s - 1, r).wait_recv()
                total = total + got_down[s - 1, part(r)].astype(jnp.float32)
            sum_down[s, part(r)] = total.astype(jnp.bfloat16)
            red_down(s, r).start()

    def finish(r):
        red_up(far - 1, r).wait_recv()
        red_down(near - 1, r).wait_recv()
        total = chip_sum(r, 0)
        total = total + got_up[far - 1, part(r)].astype(jnp.float32)
        total = total + got_down[near - 1, part(r)].astype(jnp.float32)
        out_ref[part(r)] = total.astype(out_ref.dtype)

    last = 2 * far + 2
    for r in range(regions):
        gather_step(0, r)
    for t in range(1, last + regions):
        for r in range(regions):
            stage = t - r
            if 1 <= stage <= far:
                gather_step(stage, r)
            elif far + 2 <= stage < last:
                reduce_step(stage - far - 2, r)
            elif stage == last:
                finish(r)
        if 0 <= t - far - 1 < regions:
            compute(t - far - 1)

    for r in range(regions):
        for a in range(far):
            up_hop(a, r).wait_send()
            red_up(a, r).wait_send()
        for a in range(near):
            down_hop(a, r).wait_send()
            red_down(a, r).wait_send()
        for i in range(ring):
            side(i, r).wait_send()
        swap(r).wait_send()


def over_batch(fetched, basis_values, weights, batch_count):
    ring = batch_count // 2
    far = ring // 2
    near = ring - 1 - far
    regions = basis_values.shape[0]
    requests, rows, width = fetched.shape
    dma = pltpu.SemaphoreType.DMA
    half = jnp.bfloat16
    vmem = pl.BlockSpec(memory_space=pltpu.VMEM)
    return pl.pallas_call(
        functools.partial(batch_kernel, ring, far, regions, rows),
        out_shape=jax.ShapeDtypeStruct((requests, rows, width), half),
        in_specs=[vmem] * 3,
        out_specs=vmem,
        scratch_shapes=[
            pltpu.VMEM((requests, batch_count, rows, width), half),
            pltpu.VMEM((requests, ring, 2, rows, width), half),
            pltpu.VMEM((requests, ring, rows, width), half),
            pltpu.VMEM((far, requests, rows, width), half),
            pltpu.VMEM((far, requests, rows, width), half),
            pltpu.VMEM((near, requests, rows, width), half),
            pltpu.VMEM((near, requests, rows, width), half),
            dma((far, regions)), dma((far, regions)),
            dma((near, regions)), dma((near, regions)),
            dma((ring, regions)), dma((ring, regions)),
            dma((regions,)), dma((regions,)),
            dma((far, regions)), dma((far, regions)),
            dma((near, regions)), dma((near, regions)),
        ],
        compiler_params=pltpu.CompilerParams(
            collective_id=0, has_side_effects=True, vmem_limit_bytes=48 * 1024 * 1024
        ),
        name="over_batch",
    )(fetched, basis_values, weights)


def shards(basis_values, dens_tiles, region_tiles, point_counts, point_weights):
    owner_count = lax.axis_size("region")
    batch_count = lax.axis_size("batch")
    my_index = lax.axis_index("region")
    region_local = basis_values.shape[0]
    point_local = basis_values.shape[2]
    tile_local = dens_tiles.shape[0]
    requests = 3 * region_local
    owners = region_tiles.reshape(owner_count, requests) // tile_local
    local_ids = region_tiles.reshape(owner_count, requests) % tile_local
    tile_ids = jnp.arange(tile_local, dtype=jnp.int32)
    chosen = (owners == my_index)[:, :, None] & (local_ids[:, :, None] == tile_ids)
    selector = jnp.sum(chosen.astype(jnp.float32), axis=1).astype(jnp.bfloat16)
    my_owners = lax.dynamic_index_in_dim(owners, my_index, 0, keepdims=False)
    outgoing = jnp.einsum(
        "dt,trb->drb", selector, dens_tiles, preferred_element_type=jnp.float32
    ).astype(jnp.bfloat16)
    incoming = lax.all_to_all(outgoing, "region", split_axis=0, concat_axis=0, tiled=True)
    fetched = jnp.take(incoming, my_owners, axis=0)
    live = jnp.arange(point_local, dtype=jnp.int32)[None, :] < point_counts
    weights = jnp.where(live, point_weights, 0.0)[:, :, None]
    pairs = over_batch(fetched, basis_values, weights, batch_count)
    placement = (
        my_owners[:, None] == jnp.arange(owner_count, dtype=jnp.int32)[None, :]
    ).astype(jnp.bfloat16)
    outgoing_sums = jnp.einsum(
        "jd,jrb->drb", placement, pairs, preferred_element_type=jnp.float32
    ).astype(jnp.bfloat16)
    returned = lax.all_to_all(outgoing_sums, "region", split_axis=0, concat_axis=0, tiled=True)
    return jnp.einsum("dt,drb->trb", selector, returned, preferred_element_type=jnp.float32)


def solution(mesh):
    return jax.shard_map(
        shards,
        mesh=mesh,
        in_specs=(
            P("region", None, "batch", None),
            P("region", "batch", None),
            P(),
            P("region", "batch"),
            P("region", "batch"),
        ),
        out_specs=P("region", "batch", None),
        check_vma=False,
    )
```

time: 331 us -> 159 us (0.48)
  the two profiles are of different devices: /device:TPU:1 before, /device:TPU:24 now
where the time goes in v1:
time: 159 us
  Pallas kernels  76.4 us (48%)
  blocking collectives  32.8 us (21%)
  waiting for transfers between devices  28.1 us (18%)
  starting transfers between devices  13.4 us (8%)
  local copies, waits for them, and re-layouts  6.18 us (4%)
  matrix products  1.72 us (1%)
    pallas_call x1, Pallas kernels, over_batch(): pl.pallas_call(functools.partial(batch_kernel, ring, far, regions, rows),...  76.4 us
    all_to_all x1, blocking collectives, shards(): lax.all_to_all(outgoing_sums, 'region', split_axis=0, concat_axis=0, tile...  32.8 us
    all_to_all x1, waiting for transfers between devices, shards(): lax.all_to_all(outgoing, 'region', split_axis=0, concat_axis=0, tiled=True)  28.1 us
    all_to_all x1, starting transfers between devices, shards(): lax.all_to_all(outgoing, 'region', split_axis=0, concat_axis=0, tiled=True)  13.4 us
  transfers between devices with their start and end apart: 1, of which 1 were waited for; matrix products, arithmetic and copies ran while one was open for 0% of the time, Pallas kernels for 0%

profile of v1, /device:TPU:24, one launch (start us, length us, event | category | flops | bytes accessed | tf_op | source)
XLA Modules:
  0.0 158.9 jit_solution(15424069035607639391)
XLA Ops:
  0.0 0.0 copy-start
  0.0 0.8 copy.55
  0.8 0.1 reshape.90
  0.9 0.1 copy.56
  1.1 0.0 copy-done
  1.1 0.5 convolution_convert_fusion
  1.6 0.0 copy-start.2
  1.6 0.0 copy-start.3
  1.6 1.6 %copy.61 = bf16[32,32,512]{2,1,0:T(8,128)(2,1)} copy(bf16[32,32,512]{2,0,1:T(8,128)(2,1)S(1)} %convolution_convert_fusion) | data formatting | bytes 2097152 | tf_op jit(solution)/shard_map/convert_element_type | solution.py:252
  3.2 0.0 copy-start.1
  3.2 13.4 %all-to-all-start = ((bf16[32,32,512]{2,1,0:T(8,128)(2,1)}), bf16[32,32,512]{2,1,0:T(8,128)(2,1)}, u32[]{:S(2)}, u32[]{:S(2)}) async-start(bf16[32,32,512]{2,1,0:T(8,128)(2,1)} %copy.61), calls=%async_computation | async-start | bytes 2097152 | tf_op jit(solution)/shard_map/all_to_all | solution.py:253
  16.6 0.0 copy-done.2
  16.6 0.0 copy-done.3
  16.6 0.1 select_bitcast_fusion
  16.7 0.2 copy.62.weight_ref
  16.9 0.2 dynamic-slice_reduce_fusion
  17.2 28.1 %all-to-all-done = bf16[32,32,512]{2,1,0:T(8,128)(2,1)} async-done(((bf16[32,32,512]{2,1,0:T(8,128)(2,1)}), bf16[32,32,512]{2,1,0:T(8,128)(2,1)}, u32[]{:S(2)}, u32[]{:S(2)}) %all-to-all-start) | async-done | bytes 1048608 | tf_op jit(solution)/shard_map/all_to_all | solution.py:253
  45.2 1.8 %gather_fusion = bf16[12,32,512]{2,1,0:T(8,128)(2,1)S(1)} fusion(bf16[32,32,512]{2,1,0:T(8,128)(2,1)} %all-to-all-done, s32[1024]{0:T(1024)S(1)} %pad_clamp_fusion), kind=kCustom, calls=%fused_computation | custom fusion | bytes 786480 | tf_op jit(solution)/shard_map/jit(_take)/gather | solution.py:254
  47.0 0.1 broadcast_select_fusion.own_ref
  47.1 0.0 copy-done.1
  47.2 76.4 %over_batch.1 = bf16[12,32,512]{2,1,0:T(8,128)(2,1)S(1)} custom-call(bf16[12,32,512]{2,1,0:T(8,128)(2,1)S(1)} %broadcast_select_fusion.own_ref, bf16[4,2,256,512]{3,2,1,0:T(8,128)(2,1)S(1)} %copy-done.1, f32[4,256,1]{2,1,0:T(8,128)S(1)} %copy.62.weight_ref), custom_call_target="tpu_custom_call" | custom-call | tf_op jit(solution)/shard_map/over_batch/pallas_call | solution.py:209
  123.5 0.6 convolution_convert_fusion.1
  124.1 0.6 copy.64
  124.7 32.8 %all_to_all.10 = bf16[32,32,512]{2,1,0:T(8,128)(2,1)S(1)} all-to-all(bf16[32,32,512]{2,1,0:T(8,128)(2,1)S(1)} %copy.64), channel_id=1, replica_groups=mesh['region'=32,'batch'=16] {'region'}, dimensions={0} | all-to-all | bytes 2097152 | tf_op jit(solution)/shard_map/all_to_all | solution.py:264
  157.5 0.7 fusion
  158.1 0.8 copy.66
  (6 shorter events, 0.1 us)
Async XLA Ops:
  0.0 1.1 copy-start
  1.6 15.1 %copy-start.2 = (f32[4,256]{1,0:T(4,128)S(1)}, f32[4,256]{1,0:T(4,128)}, u32[]{:S(2)}) copy-start(f32[4,256]{1,0:T(4,128)} %param.9) | copy-start | bytes 12292
  1.6 15.1 %copy-start.3 = (s32[4,1]{0,1:T(1,128)S(1)}, s32[4,1]{0,1:T(1,128)}, u32[]{:S(2)}) copy-start(s32[4,1]{0,1:T(1,128)} %param.8) | copy-start | bytes 52
  3.2 44.0 %copy-start.1 = (bf16[4,2,256,512]{3,2,1,0:T(8,128)(2,1)S(1)}, bf16[4,2,256,512]{3,2,1,0:T(8,128)(2,1)}, u32[]{:S(2)}) copy-start(bf16[4,2,256,512]{3,2,1,0:T(8,128)(2,1)} %phi_ref.1) | copy-start | bytes 6291460
  3.2 42.0 %all-to-all-start = ((bf16[32,32,512]{2,1,0:T(8,128)(2,1)}), bf16[32,32,512]{2,1,0:T(8,128)(2,1)}, u32[]{:S(2)}, u32[]{:S(2)}) async-start(bf16[32,32,512]{2,1,0:T(8,128)(2,1)} %copy.61), calls=%async_computation | async-start | bytes 2097152 | tf_op jit(solution)/shard_map/all_to_all | solution.py:253

commit v2 on v1

--- a/solution.py
+++ b/solution.py
@@ -233,9 +233,254 @@
     )(fetched, basis_values, weights)
 
 
+def plane(columns, ring):
+    m = lax.axis_index("region")
+    x, z = m // ring, m % ring
+    way = 1 - 2 * (lax.axis_index("batch") % 2)
+
+    def at(k):
+        return lax.rem(z + k * way + ring, ring)
+
+    def along_z(k):
+        return x * ring + at(k)
+
+    def along_x(d):
+        return lax.rem(x + d, columns) * ring + z
+
+    def greet():
+        barrier = pltpu.get_barrier_semaphore()
+        targets = [along_z(1), along_z(-1)] + [along_x(d) for d in range(1, columns)]
+        for target in targets:
+            pl.semaphore_signal(barrier, inc=1, device_id={"region": target}, device_id_type=MESH)
+        pl.semaphore_wait(barrier, len(targets))
+
+    return m, x, z, at, along_z, along_x, greet
+
+
+def to_region(src, dst, send, recv, target):
+    return pltpu.make_async_remote_copy(
+        src_ref=src, dst_ref=dst, send_sem=send, recv_sem=recv,
+        device_id={"region": target}, device_id_type=MESH,
+    )
+
+
+def fetch_kernel(columns, ring, far, table_ref, owner_ref, own_ref, out_ref, stage, landed,
+                 up_send, up_recv, down_send, down_recv, x_send, x_recv, *held):
+    near = ring - 1 - far
+    kept = own_ref.shape[0]
+    m, x, z, at, along_z, along_x, greet = plane(columns, ring)
+    greet()
+
+    def source(i):
+        return own_ref if i == 0 else held[i - 1]
+
+    def place(i):
+        return 0 if i == 0 else (-i if i <= far else i - far)
+
+    def up(a, t):
+        return to_region(source(a).at[t], held[a].at[t], up_send.at[a, t], up_recv.at[a, t], along_z(1))
+
+    def down(a, t):
+        src = own_ref if a == 0 else held[far + a - 1]
+        return to_region(
+            src.at[t], held[far + a].at[t], down_send.at[a, t], down_recv.at[a, t], along_z(-1)
+        )
+
+    def across(d, i):
+        return to_region(
+            stage.at[d - 1, i], landed.at[along_z(place(i))],
+            x_send.at[d - 1, i], x_recv.at[d - 1, i], along_x(d),
+        )
+
+    def arrival(d, i):
+        slot = landed.at[lax.rem(x + columns - d, columns) * ring + at(place(i))]
+        return to_region(slot, slot, x_send.at[d - 1, i], x_recv.at[d - 1, i], along_x(d))
+
+    def pass_on(i):
+        zo = at(place(i))
+        for d in range(1, columns):
+            wanted = jnp.maximum(table_ref[lax.rem(x + d, columns), zo], 0)
+            stage[d - 1, i] = source(i)[wanted]
+            across(d, i).start()
+        landed[along_z(place(i))] = source(i)[jnp.maximum(table_ref[x, zo], 0)]
+
+    for t in range(kept):
+        up(0, t).start()
+        down(0, t).start()
+    pass_on(0)
+    for a in range(1, far + 1):
+        for t in range(kept):
+            up(a - 1, t).wait_recv()
+            if a < far:
+                up(a, t).start()
+            if a <= near:
+                down(a - 1, t).wait_recv()
+                if a < near:
+                    down(a, t).start()
+        pass_on(a)
+        if a <= near:
+            pass_on(far + a)
+    for i in range(ring):
+        for d in range(1, columns):
+            arrival(d, i).wait_recv()
+    for j in range(out_ref.shape[0]):
+        out_ref[j] = landed[owner_ref[j]]
+    for t in range(kept):
+        for a in range(far):
+            up(a, t).wait_send()
+        for a in range(near):
+            down(a, t).wait_send()
+    for i in range(ring):
+        for d in range(1, columns):
+            across(d, i).wait_send()
+
+
+def give_kernel(columns, ring, far, table_ref, request_ref, pairs_ref, out_ref, stage, landed,
+                sum_up, got_up, sum_down, got_down,
+                up_send, up_recv, down_send, down_recv, x_send, x_recv):
+    near = ring - 1 - far
+    kept = out_ref.shape[0]
+    m, x, z, at, along_z, along_x, greet = plane(columns, ring)
+    greet()
+
+    def across(d, i):
+        return to_region(
+            stage.at[d - 1, i], landed.at[d - 1, i], x_send.at[d - 1, i], x_recv.at[d - 1, i], along_x(d)
+        )
+
+    def up(s, t):
+        return to_region(sum_up.at[s, t], got_up.at[s, t], up_send.at[s, t], up_recv.at[s, t], along_z(1))
+
+    def down(s, t):
+        return to_region(
+            sum_down.at[s, t], got_down.at[s, t], down_send.at[s, t], down_recv.at[s, t], along_z(-1)
+        )
+
+    order = []
+    for s in range(far):
+        order.append(far - s)
+        if s < near:
+            order.append(s - near)
+    order.append(0)
+    for k in order:
+        for d in range(1, columns):
+            request = request_ref[lax.rem(x + d, columns), at(k)]
+            stage[d - 1, k % ring] = pairs_ref[request]
+            across(d, k % ring).start()
+
+    def placed(k):
+        for d in range(1, columns):
+            across(d, k % ring).wait_recv()
+        terms = [(table_ref[x, at(k)], pairs_ref[request_ref[x, at(k)]].astype(jnp.float32))]
+        for d in range(1, columns):
+            sender = lax.rem(x + columns - d, columns)
+            terms.append((table_ref[sender, at(k)], landed[d - 1, k % ring].astype(jnp.float32)))
+
+        def tile(t):
+            total = jnp.zeros(pairs_ref.shape[1:], jnp.float32)
+            for wanted, values in terms:
+                total = total + jnp.where(jnp.full(values.shape, wanted, jnp.int32) == t, values, 0.0)
+            return total
+
+        return tile
+
+    for s in range(far):
+        tile = placed(far - s)
+        for t in range(kept):
+            total = tile(t)
+            if s > 0:
+                up(s - 1, t).wait_recv()
+                total = total + got_up[s - 1, t].astype(jnp.float32)
+            sum_up[s, t] = total.astype(sum_up.dtype)
+            up(s, t).start()
+        if s < near:
+            tile = placed(s - near)
+            for t in range(kept):
+                total = tile(t)
+                if s > 0:
+                    down(s - 1, t).wait_recv()
+                    total = total + got_down[s - 1, t].astype(jnp.float32)
+                sum_down[s, t] = total.astype(sum_down.dtype)
+                down(s, t).start()
+    tile = placed(0)
+    for t in range(kept):
+        total = tile(t)
+        down(near - 1, t).wait_recv()
+        total = total + got_down[near - 1, t].astype(jnp.float32)
+        up(far - 1, t).wait_recv()
+        out_ref[t] = total + got_up[far - 1, t].astype(jnp.float32)
+    for t in range(kept):
+        for s in range(far):
+            up(s, t).wait_send()
+        for s in range(near):
+            down(s, t).wait_send()
+    for k in order:
+        for d in range(1, columns):
+            across(d, k % ring).wait_send()
+
+
+def over_region(kernel, name, collective_id, scratch, out, columns, ring, far, table, index, values):
+    vmem, smem = pl.BlockSpec(memory_space=pltpu.VMEM), pl.BlockSpec(memory_space=pltpu.SMEM)
+    return pl.pallas_call(
+        functools.partial(kernel, columns, ring, far),
+        out_shape=out,
+        in_specs=[smem, smem, vmem],
+        out_specs=vmem,
+        scratch_shapes=scratch,
+        compiler_params=pltpu.CompilerParams(
+            collective_id=collective_id, has_side_effects=True, vmem_limit_bytes=32 * 1024 * 1024
+        ),
+        name=name,
+    )(table, index, values)
+
+
+COLUMNS = 4
+
+
+def plane_semaphores(columns, ring, far, kept):
+    dma = pltpu.SemaphoreType.DMA
+    near = ring - 1 - far
+    return [
+        dma((far, kept)), dma((far, kept)), dma((near, kept)), dma((near, kept)),
+        dma((columns - 1, ring)), dma((columns - 1, ring)),
+    ]
+
+
+def fetch(table, my_owners, dens_tiles, ring):
+    far = ring // 2
+    kept, rows, width = dens_tiles.shape
+    kind = dens_tiles.dtype
+    scratch = [
+        pltpu.VMEM((COLUMNS - 1, ring, rows, width), kind),
+        pltpu.VMEM((COLUMNS * ring, rows, width), kind),
+    ]
+    scratch += plane_semaphores(COLUMNS, ring, far, kept)
+    scratch += [pltpu.VMEM((kept, rows, width), kind)] * (ring - 1)
+    out = jax.ShapeDtypeStruct((my_owners.shape[0], rows, width), kind)
+    return over_region(
+        fetch_kernel, "fetch", 1, scratch, out, COLUMNS, ring, far, table, my_owners, dens_tiles
+    )
+
+
+def give(table, request, pairs, kept, ring):
+    far = ring // 2
+    near = ring - 1 - far
+    rows, width = pairs.shape[1:]
+    kind = pairs.dtype
+    scratch = [pltpu.VMEM((COLUMNS - 1, ring, rows, width), kind)] * 2
+    scratch += [pltpu.VMEM((far, kept, rows, width), kind)] * 2
+    scratch += [pltpu.VMEM((near, kept, rows, width), kind)] * 2
+    scratch += plane_semaphores(COLUMNS, ring, far, kept)
+    out = jax.ShapeDtypeStruct((kept, rows, width), jnp.float32)
+    return over_region(
+        give_kernel, "give", 2, scratch, out, COLUMNS, ring, far, table, request, pairs
+    )
+
+
 def shards(basis_values, dens_tiles, region_tiles, point_counts, point_weights):
     owner_count = lax.axis_size("region")
     batch_count = lax.axis_size("batch")
+    ring = owner_count // COLUMNS
     my_index = lax.axis_index("region")
     region_local = basis_values.shape[0]
     point_local = basis_values.shape[2]
@@ -243,26 +488,21 @@
     requests = 3 * region_local
     owners = region_tiles.reshape(owner_count, requests) // tile_local
     local_ids = region_tiles.reshape(owner_count, requests) % tile_local
-    tile_ids = jnp.arange(tile_local, dtype=jnp.int32)
-    chosen = (owners == my_index)[:, :, None] & (local_ids[:, :, None] == tile_ids)
-    selector = jnp.sum(chosen.astype(jnp.float32), axis=1).astype(jnp.bfloat16)
+    mine = owners[:, :, None] == jnp.arange(owner_count, dtype=jnp.int32)
+    wanted = jnp.sum(jnp.where(mine, local_ids[:, :, None] + 1, 0), axis=1) - 1
+    order = jnp.arange(requests, dtype=jnp.int32)
+    request_of = jnp.sum(jnp.where(mine, order[None, :, None], 0), axis=1)
     my_owners = lax.dynamic_index_in_dim(owners, my_index, 0, keepdims=False)
-    outgoing = jnp.einsum(
-        "dt,trb->drb", selector, dens_tiles, preferred_element_type=jnp.float32
-    ).astype(jnp.bfloat16)
-    incoming = lax.all_to_all(outgoing, "region", split_axis=0, concat_axis=0, tiled=True)
-    fetched = jnp.take(incoming, my_owners, axis=0)
+    request = lax.dynamic_index_in_dim(request_of, my_index, 0, keepdims=False)
+    request = request.reshape(COLUMNS, ring)
+    table = wanted.reshape(COLUMNS, ring, COLUMNS, ring)
+    table = lax.dynamic_index_in_dim(table, my_index % ring, 1, keepdims=False)
+    table = lax.dynamic_index_in_dim(table, my_index // ring, 1, keepdims=False)
+    fetched = fetch(table, my_owners, dens_tiles, ring)
     live = jnp.arange(point_local, dtype=jnp.int32)[None, :] < point_counts
     weights = jnp.where(live, point_weights, 0.0)[:, :, None]
     pairs = over_batch(fetched, basis_values, weights, batch_count)
-    placement = (
-        my_owners[:, None] == jnp.arange(owner_count, dtype=jnp.int32)[None, :]
-    ).astype(jnp.bfloat16)
-    outgoing_sums = jnp.einsum(
-        "jd,jrb->drb", placement, pairs, preferred_element_type=jnp.float32
-    ).astype(jnp.bfloat16)
-    returned = lax.all_to_all(outgoing_sums, "region", split_axis=0, concat_axis=0, tiled=True)
-    return jnp.einsum("dt,drb->trb", selector, returned, preferred_element_type=jnp.float32)
+    return give(table, request, pairs, tile_local, ring)
 
 
 def solution(mesh):

time: 159 us -> 140 us (0.88)
  the two profiles are of different devices: /device:TPU:24 before, /device:TPU:8 now
where the time goes in v2:
time: 140 us
  Pallas kernels  134 us (96%)
  local copies, waits for them, and re-layouts  4.77 us (3%)
    pallas_call x1, Pallas kernels, over_batch(): pl.pallas_call(functools.partial(batch_kernel, ring, far, regions, rows),...  76.8 us
    pallas_call x2, Pallas kernels, over_region(): pl.pallas_call(functools.partial(kernel, columns, ring, far), out_shape=o...  56.9 us
    unnamed x6, local copies, waits for them, and re-layouts  3.98 us

profile of v2, /device:TPU:8, one launch (start us, length us, event | category | flops | bytes accessed | tf_op | source)
XLA Modules:
  0.0 139.5 jit_solution(4929390110864501917)
XLA Ops:
  0.0 0.8 select_bitcast_fusion
  0.8 0.8 copy.18
  1.5 0.1 reshape.65
  1.6 0.1 copy.19
  1.7 0.2 dynamic-slice_reduce_fusion.owner_ref
  1.9 0.2 select_reduce_fusion
  2.1 0.1 reshape.66.request_ref
  2.2 0.1 sub.18
  2.3 0.0 copy-start.1
  2.4 0.9 copy-done.1
  3.2 32.3 %fetch.1.own_ref = bf16[12,32,512]{2,1,0:T(8,128)(2,1)S(1)} custom-call(s32[4,8]{1,0:T(4,128)S(1)} %bitcast.4, s32[12]{0:T(128)S(1)} %dynamic-slice_reduce_fusion.owner_ref, bf16[4,32,512]{2,1,0:T(8,128)(2,1)S(1)} %copy-done.1), custom_call_target="tpu_custom_call" | custom-call | tf_op jit(solution)/shard_map/fetch/pallas_call | solution.py:424
  35.6 0.2 copy.23.weight_ref
  35.8 0.0 copy-start
  35.8 1.6 %copy-done = bf16[4,2,256,512]{3,2,1,0:T(8,128)(2,1)S(1)} copy-done((bf16[4,2,256,512]{3,2,1,0:T(8,128)(2,1)S(1)}, bf16[4,2,256,512]{3,2,1,0:T(8,128)(2,1)}, u32[]{:S(2)}) %copy-start) | copy-done | bytes 2097176
  37.4 76.8 %over_batch.1.pairs_ref = bf16[12,32,512]{2,1,0:T(8,128)(2,1)S(1)} custom-call(bf16[12,32,512]{2,1,0:T(8,128)(2,1)S(1)} %fetch.1.own_ref, bf16[4,2,256,512]{3,2,1,0:T(8,128)(2,1)S(1)} %copy-done, f32[4,256,1]{2,1,0:T(8,128)S(1)} %copy.23.weight_ref), custom_call_target="tpu_custom_call" | custom-call | tf_op jit(solution)/shard_map/over_batch/pallas_call | solution.py:209
  114.2 24.6 %give.1 = f32[4,32,512]{2,1,0:T(8,128)S(1)} custom-call(s32[4,8]{1,0:T(4,128)S(1)} %bitcast.5, s32[4,8]{1,0:T(4,128)S(1)} %reshape.66.request_ref, bf16[12,32,512]{2,1,0:T(8,128)(2,1)S(1)} %over_batch.1.pairs_ref), custom_call_target="tpu_custom_call" | custom-call | tf_op jit(solution)/shard_map/give/pallas_call | solution.py:424
  138.8 0.7 copy.25
  (4 shorter events, 0.1 us)
Async XLA Ops:
  2.3 0.9 copy-start.1
  35.8 1.6 %copy-start = (bf16[4,2,256,512]{3,2,1,0:T(8,128)(2,1)S(1)}, bf16[4,2,256,512]{3,2,1,0:T(8,128)(2,1)}, u32[]{:S(2)}) copy-start(bf16[4,2,256,512]{3,2,1,0:T(8,128)(2,1)} %phi_ref.1) | copy-start | bytes 6291460

commit v3 on v2

--- a/solution.py
+++ b/solution.py
@@ -15,9 +15,31 @@
     return -SLATER * density * jnp.exp(jnp.log(density * density + 1.0) * (-1.0 / 3.0))
 
 
+GATHER, COMPUTE, REDUCE, FINISH = range(4)
+
+
+def schedule(far, near, regions):
+    if (far, regions) != (4, 4):
+        order = [(GATHER, a, r) for a in range(far + 1) for r in range(regions)]
+        order += [(COMPUTE, r) for r in range(regions)]
+        order += [(REDUCE, s, r) for s in range(far) for r in range(regions)]
+        return order + [(FINISH, r) for r in range(regions)]
+    order = []
+    for t in range(5):
+        order += [(GATHER, t, 0), (GATHER, t, 1)]
+        if t >= 2:
+            order += [(GATHER, t - 2, 2), (GATHER, t - 2, 3)]
+    order += [(COMPUTE, 0), (GATHER, 3, 2), (GATHER, 3, 3), (COMPUTE, 1), (REDUCE, 0, 0)]
+    order += [(GATHER, 4, 2), (REDUCE, 0, 1), (GATHER, 4, 3), (REDUCE, 1, 0), (COMPUTE, 2)]
+    order += [(REDUCE, 1, 1), (REDUCE, 2, 0), (REDUCE, 0, 2), (COMPUTE, 3), (REDUCE, 1, 2)]
+    order += [(REDUCE, 2, 1), (REDUCE, 3, 0), (REDUCE, 0, 3), (REDUCE, 2, 2), (REDUCE, 3, 1)]
+    order += [(REDUCE, 1, 3), (FINISH, 0), (REDUCE, 3, 2), (REDUCE, 2, 3), (FINISH, 1)]
+    return order + [(REDUCE, 3, 3), (FINISH, 2), (FINISH, 3)]
+
+
 def batch_kernel(
-    ring, far, regions, rows, own_ref, phi_ref, weight_ref, out_ref,
-    tiles, pairs, peer, sum_up, got_up, sum_down, got_down,
+    ring, far, regions, rows, own_ref, basis_ref, weight_ref, out_ref,
+    phi_ref, load, tiles, pairs, peer, sum_up, got_up, sum_down, got_down,
     up_send, up_recv, down_send, down_recv, side_send, side_recv,
     swap_send, swap_recv, red_up_send, red_up_recv, red_down_send, red_down_recv,
 ):
@@ -36,6 +58,11 @@
     def theirs(k):
         return at(k) * 2 + (1 - c)
 
+    def values(r):
+        return pltpu.make_async_copy(basis_ref.at[r], phi_ref.at[r], load.at[r])
+
+    for r in range(regions):
+        values(r).start()
     barrier = pltpu.get_barrier_semaphore()
     for target in (mine(1), mine(-1), other):
         pl.semaphore_signal(barrier, inc=1, device_id={"batch": target}, device_id_type=MESH)
@@ -108,12 +135,13 @@
     def compute(r):
         for i in range(ring):
             side_arrival(i, r).wait_recv()
+        values(r).wait()
         width = phi_ref.shape[-1]
         phi_a, phi_b = phi_ref[r, 0], phi_ref[r, 1]
 
-        def left(values, j):
+        def left(phi, j):
             matrix = tiles[3 * r + j].reshape(2 * ring * rows, width)
-            return jnp.dot(values, matrix, preferred_element_type=jnp.float32)
+            return jnp.dot(phi, matrix, preferred_element_type=jnp.float32)
 
         wide_a, wide_b = phi_a.astype(jnp.float32), phi_b.astype(jnp.float32)
         density = jnp.sum(
@@ -170,20 +198,8 @@
         total = total + got_down[near - 1, part(r)].astype(jnp.float32)
         out_ref[part(r)] = total.astype(out_ref.dtype)
 
-    last = 2 * far + 2
-    for r in range(regions):
-        gather_step(0, r)
-    for t in range(1, last + regions):
-        for r in range(regions):
-            stage = t - r
-            if 1 <= stage <= far:
-                gather_step(stage, r)
-            elif far + 2 <= stage < last:
-                reduce_step(stage - far - 2, r)
-            elif stage == last:
-                finish(r)
-        if 0 <= t - far - 1 < regions:
-            compute(t - far - 1)
+    for action, *where in schedule(far, near, regions):
+        (gather_step, compute, reduce_step, finish)[action](*where)
 
     for r in range(regions):
         for a in range(far):
@@ -209,9 +225,10 @@
     return pl.pallas_call(
         functools.partial(batch_kernel, ring, far, regions, rows),
         out_shape=jax.ShapeDtypeStruct((requests, rows, width), half),
-        in_specs=[vmem] * 3,
+        in_specs=[vmem, pl.BlockSpec(memory_space=pltpu.HBM), vmem],
         out_specs=vmem,
         scratch_shapes=[
+            pltpu.VMEM(basis_values.shape, half), dma((regions,)),
             pltpu.VMEM((requests, batch_count, rows, width), half),
             pltpu.VMEM((requests, ring, 2, rows, width), half),
             pltpu.VMEM((requests, ring, rows, width), half),

time: 140 us -> 138 us (0.986)
  the two profiles are of different devices: /device:TPU:8 before, /device:TPU:4 now
where the time goes in v3:
time: 138 us; the launch traced here: 137 us
  Pallas kernels  132 us (96%)
  local copies, waits for them, and re-layouts  4.77 us (3%)
    pallas_call x1, Pallas kernels, over_batch(): pl.pallas_call(functools.partial(batch_kernel, ring, far, regions, rows),...  76.9 us
    pallas_call x2, Pallas kernels, over_region(): pl.pallas_call(functools.partial(kernel, columns, ring, far), out_shape=o...  54.8 us
    unnamed x6, local copies, waits for them, and re-layouts  3.98 us

profile of v3, /device:TPU:4, one launch (start us, length us, event | category | flops | bytes accessed | tf_op | source)
XLA Modules:
  0.0 137.5 jit_solution(11041601208202062008)
XLA Ops:
  0.0 0.8 select_bitcast_fusion
  0.8 0.8 copy.18
  1.5 0.1 reshape.65
  1.6 0.1 copy.19
  1.7 0.2 dynamic-slice_reduce_fusion.owner_ref
  1.9 0.2 select_reduce_fusion
  2.1 0.1 reshape.66.request_ref
  2.2 0.1 sub.18
  2.3 0.0 copy-start.1
  2.4 0.9 copy-done.1
  3.2 30.8 %fetch.1.own_ref = bf16[12,32,512]{2,1,0:T(8,128)(2,1)S(1)} custom-call(s32[4,8]{1,0:T(4,128)S(1)} %bitcast.4, s32[12]{0:T(128)S(1)} %dynamic-slice_reduce_fusion.owner_ref, bf16[4,32,512]{2,1,0:T(8,128)(2,1)S(1)} %copy-done.1), custom_call_target="tpu_custom_call" | custom-call | tf_op jit(solution)/shard_map/fetch/pallas_call | solution.py:441
  34.1 0.2 copy.23.weight_ref
  34.3 0.0 copy-start
  34.3 1.6 %copy-done = bf16[4,2,256,512]{3,2,1,0:T(8,128)(2,1)S(1)} copy-done((bf16[4,2,256,512]{3,2,1,0:T(8,128)(2,1)S(1)}, bf16[4,2,256,512]{3,2,1,0:T(8,128)(2,1)}, u32[]{:S(2)}) %copy-start) | copy-done | bytes 2097176
  35.9 76.9 %over_batch.1.pairs_ref = bf16[12,32,512]{2,1,0:T(8,128)(2,1)S(1)} custom-call(bf16[12,32,512]{2,1,0:T(8,128)(2,1)S(1)} %fetch.1.own_ref, bf16[4,2,256,512]{3,2,1,0:T(8,128)(2,1)S(1)} %copy-done, f32[4,256,1]{2,1,0:T(8,128)S(1)} %copy.23.weight_ref), custom_call_target="tpu_custom_call" | custom-call | tf_op jit(solution)/shard_map/over_batch/pallas_call | solution.py:225
  112.8 24.0 %give.1 = f32[4,32,512]{2,1,0:T(8,128)S(1)} custom-call(s32[4,8]{1,0:T(4,128)S(1)} %bitcast.5, s32[4,8]{1,0:T(4,128)S(1)} %reshape.66.request_ref, bf16[12,32,512]{2,1,0:T(8,128)(2,1)S(1)} %over_batch.1.pairs_ref), custom_call_target="tpu_custom_call" | custom-call | tf_op jit(solution)/shard_map/give/pallas_call | solution.py:441
  136.8 0.7 copy.25
  (4 shorter events, 0.1 us)
Async XLA Ops:
  2.3 0.9 copy-start.1
  34.3 1.6 %copy-start = (bf16[4,2,256,512]{3,2,1,0:T(8,128)(2,1)S(1)}, bf16[4,2,256,512]{3,2,1,0:T(8,128)(2,1)}, u32[]{:S(2)}) copy-start(bf16[4,2,256,512]{3,2,1,0:T(8,128)(2,1)} %basis_ref.1) | copy-start | bytes 6291460

commit v4 on v3

--- a/solution.py
+++ b/solution.py
@@ -244,7 +244,7 @@
             dma((near, regions)), dma((near, regions)),
         ],
         compiler_params=pltpu.CompilerParams(
-            collective_id=0, has_side_effects=True, vmem_limit_bytes=48 * 1024 * 1024
+            collective_id=0, has_side_effects=True, vmem_limit_bytes=52 * 1024 * 1024
         ),
         name="over_batch",
     )(fetched, basis_values, weights)
@@ -262,7 +262,7 @@
         return x * ring + at(k)
 
     def along_x(d):
-        return lax.rem(x + d, columns) * ring + z
+        return lax.rem(x + d + columns, columns) * ring + z
 
     def greet():
         barrier = pltpu.get_barrier_semaphore()
@@ -271,7 +271,7 @@
             pl.semaphore_signal(barrier, inc=1, device_id={"region": target}, device_id_type=MESH)
         pl.semaphore_wait(barrier, len(targets))
 
-    return m, x, z, at, along_z, along_x, greet
+    return x, way, at, along_z, along_x, greet
 
 
 def to_region(src, dst, send, recv, target):
@@ -282,10 +282,11 @@
 
 
 def fetch_kernel(columns, ring, far, table_ref, owner_ref, own_ref, out_ref, stage, landed,
-                 up_send, up_recv, down_send, down_recv, x_send, x_recv, *held):
+                 up_send, up_recv, down_send, down_recv, x_send, x_recv, relay, relay_send, relay_recv,
+                 *held):
     near = ring - 1 - far
     kept = own_ref.shape[0]
-    m, x, z, at, along_z, along_x, greet = plane(columns, ring)
+    x, way, at, along_z, along_x, greet = plane(columns, ring)
     greet()
 
     def source(i):
@@ -313,12 +314,27 @@
         slot = landed.at[lax.rem(x + columns - d, columns) * ring + at(place(i))]
         return to_region(slot, slot, x_send.at[d - 1, i], x_recv.at[d - 1, i], along_x(d))
 
+    def first_leg(i):
+        return to_region(stage.at[1, i], relay.at[i], relay_send.at[i], relay_recv.at[i], along_x(way))
+
+    def second_leg(i):
+        column = lax.rem(x - way + columns, columns)
+        return to_region(
+            relay.at[i], landed.at[column * ring + at(place(i))],
+            x_send.at[1, i], x_recv.at[1, i], along_x(way),
+        )
+
+    def hand_on(i):
+        slot = relay.at[i]
+        to_region(slot, slot, relay_send.at[i], relay_recv.at[i], along_x(way)).wait_recv()
+        second_leg(i).start()
+
     def pass_on(i):
         zo = at(place(i))
         for d in range(1, columns):
             wanted = jnp.maximum(table_ref[lax.rem(x + d, columns), zo], 0)
             stage[d - 1, i] = source(i)[wanted]
-            across(d, i).start()
+            (first_leg(i) if d == 2 else across(d, i)).start()
         landed[along_z(place(i))] = source(i)[jnp.maximum(table_ref[x, zo], 0)]
 
     for t in range(kept):
@@ -337,6 +353,10 @@
         pass_on(a)
         if a <= near:
             pass_on(far + a)
+        hand_on(a - 1)
+        if a > 1:
+            hand_on(far + a - 1)
+    hand_on(far)
     for i in range(ring):
         for d in range(1, columns):
             arrival(d, i).wait_recv()
@@ -349,15 +369,16 @@
             down(a, t).wait_send()
     for i in range(ring):
         for d in range(1, columns):
-            across(d, i).wait_send()
+            (second_leg(i) if d == 2 else across(d, i)).wait_send()
+        first_leg(i).wait_send()
 
 
 def give_kernel(columns, ring, far, table_ref, request_ref, pairs_ref, out_ref, stage, landed,
                 sum_up, got_up, sum_down, got_down,
-                up_send, up_recv, down_send, down_recv, x_send, x_recv):
+                up_send, up_recv, down_send, down_recv, x_send, x_recv, relay, relay_send, relay_recv):
     near = ring - 1 - far
     kept = out_ref.shape[0]
-    m, x, z, at, along_z, along_x, greet = plane(columns, ring)
+    x, way, at, along_z, along_x, greet = plane(columns, ring)
     greet()
 
     def across(d, i):
@@ -372,6 +393,17 @@
         return to_region(
             sum_down.at[s, t], got_down.at[s, t], down_send.at[s, t], down_recv.at[s, t], along_z(-1)
         )
+
+    def first_leg(i):
+        return to_region(stage.at[1, i], relay.at[i], relay_send.at[i], relay_recv.at[i], along_x(way))
+
+    def second_leg(i):
+        return to_region(relay.at[i], landed.at[1, i], x_send.at[1, i], x_recv.at[1, i], along_x(way))
+
+    def hand_on(i):
+        slot = relay.at[i]
+        to_region(slot, slot, relay_send.at[i], relay_recv.at[i], along_x(way)).wait_recv()
+        second_leg(i).start()
 
     order = []
     for s in range(far):
@@ -383,9 +415,14 @@
         for d in range(1, columns):
             request = request_ref[lax.rem(x + d, columns), at(k)]
             stage[d - 1, k % ring] = pairs_ref[request]
-            across(d, k % ring).start()
+            (first_leg(k % ring) if d == 2 else across(d, k % ring)).start()
+    hand_on(order[0] % ring)
+    hand_on(order[1] % ring)
 
     def placed(k):
+        ahead = order.index(k) + 2
+        if ahead < ring:
+            hand_on(order[ahead] % ring)
         for d in range(1, columns):
             across(d, k % ring).wait_recv()
         terms = [(table_ref[x, at(k)], pairs_ref[request_ref[x, at(k)]].astype(jnp.float32))]
@@ -431,9 +468,10 @@
             up(s, t).wait_send()
         for s in range(near):
             down(s, t).wait_send()
-    for k in order:
-        for d in range(1, columns):
-            across(d, k % ring).wait_send()
+    for i in range(ring):
+        for d in range(1, columns):
+            (second_leg(i) if d == 2 else across(d, i)).wait_send()
+        first_leg(i).wait_send()
 
 
 def over_region(kernel, name, collective_id, scratch, out, columns, ring, far, table, index, values):
@@ -463,6 +501,11 @@
     ]
 
 
+def relay_scratch(ring, rows, width, kind):
+    dma = pltpu.SemaphoreType.DMA
+    return [pltpu.VMEM((ring, rows, width), kind), dma((ring,)), dma((ring,))]
+
+
 def fetch(table, my_owners, dens_tiles, ring):
     far = ring // 2
     kept, rows, width = dens_tiles.shape
@@ -472,6 +515,7 @@
         pltpu.VMEM((COLUMNS * ring, rows, width), kind),
     ]
     scratch += plane_semaphores(COLUMNS, ring, far, kept)
+    scratch += relay_scratch(ring, rows, width, kind)
     scratch += [pltpu.VMEM((kept, rows, width), kind)] * (ring - 1)
     out = jax.ShapeDtypeStruct((my_owners.shape[0], rows, width), kind)
     return over_region(
@@ -488,6 +532,7 @@
     scratch += [pltpu.VMEM((far, kept, rows, width), kind)] * 2
     scratch += [pltpu.VMEM((near, kept, rows, width), kind)] * 2
     scratch += plane_semaphores(COLUMNS, ring, far, kept)
+    scratch += relay_scratch(ring, rows, width, kind)
     out = jax.ShapeDtypeStruct((kept, rows, width), jnp.float32)
     return over_region(
         give_kernel, "give", 2, scratch, out, COLUMNS, ring, far, table, request, pairs

time: 138 us -> 143 us (1.036)
  the two profiles are of different devices: /device:TPU:4 before, /device:TPU:8 now
where the time goes in v4:
time: 143 us
  Pallas kernels  139 us (97%)
  local copies, waits for them, and re-layouts  3.18 us (2%)
    pallas_call x1, Pallas kernels, over_batch(): pl.pallas_call(functools.partial(batch_kernel, ring, far, regions, rows),...  75 us
    pallas_call x2, Pallas kernels, over_region(): pl.pallas_call(functools.partial(kernel, columns, ring, far), out_shape=o...  64 us

profile of v4, /device:TPU:8, one launch (start us, length us, event | category | flops | bytes accessed | tf_op | source)
XLA Modules:
  0.0 143.2 jit_solution(6214063640007715307)
XLA Ops:
  0.0 0.8 select_bitcast_fusion
  0.8 0.8 copy.18
  1.5 0.1 reshape.65
  1.6 0.1 copy.19
  1.7 0.2 dynamic-slice_reduce_fusion.owner_ref
  1.9 0.2 select_reduce_fusion
  2.1 0.1 reshape.66.request_ref
  2.2 0.1 sub.18
  2.3 0.0 copy-start
  2.4 0.9 copy-done
  3.2 34.9 %fetch.1.own_ref = bf16[12,32,512]{2,1,0:T(8,128)(2,1)S(1)} custom-call(s32[4,8]{1,0:T(4,128)S(1)} %bitcast.4, s32[12]{0:T(128)S(1)} %dynamic-slice_reduce_fusion.owner_ref, bf16[4,32,512]{2,1,0:T(8,128)(2,1)S(1)} %copy-done), custom_call_target="tpu_custom_call" | custom-call | tf_op jit(solution)/shard_map/fetch/pallas_call | solution.py:479
  38.2 0.2 copy.23.weight_ref
  38.4 75.0 %over_batch.1.pairs_ref = bf16[12,32,512]{2,1,0:T(8,128)(2,1)S(1)} custom-call(bf16[12,32,512]{2,1,0:T(8,128)(2,1)S(1)} %fetch.1.own_ref, bf16[4,2,256,512]{3,2,1,0:T(8,128)(2,1)} %basis_ref.1, f32[4,256,1]{2,1,0:T(8,128)S(1)} %copy.23.weight_ref), custom_call_target="tpu_custom_call" | custom-call | tf_op jit(solution)/shard_map/over_batch/pallas_call | solution.py:225
  113.4 29.1 %give.1 = f32[4,32,512]{2,1,0:T(8,128)S(1)} custom-call(s32[4,8]{1,0:T(4,128)S(1)} %bitcast.5, s32[4,8]{1,0:T(4,128)S(1)} %reshape.66.request_ref, bf16[12,32,512]{2,1,0:T(8,128)(2,1)S(1)} %over_batch.1.pairs_ref), custom_call_target="tpu_custom_call" | custom-call | tf_op jit(solution)/shard_map/give/pallas_call | solution.py:479
  142.5 0.7 copy.25
  (4 shorter events, 0.1 us)
Async XLA Ops:
  2.3 0.9 copy-start

commit v5 on v3

--- a/solution.py
+++ b/solution.py
@@ -63,11 +63,6 @@
 
     for r in range(regions):
         values(r).start()
-    barrier = pltpu.get_barrier_semaphore()
-    for target in (mine(1), mine(-1), other):
-        pl.semaphore_signal(barrier, inc=1, device_id={"batch": target}, device_id_type=MESH)
-    pl.semaphore_wait(barrier, 3)
-
     def remote(src, dst, send, recv, target):
         return pltpu.make_async_remote_copy(
             src_ref=src, dst_ref=dst, send_sem=send, recv_sem=recv,
@@ -201,53 +196,44 @@
     for action, *where in schedule(far, near, regions):
         (gather_step, compute, reduce_step, finish)[action](*where)
 
-    for r in range(regions):
-        for a in range(far):
-            up_hop(a, r).wait_send()
-            red_up(a, r).wait_send()
-        for a in range(near):
-            down_hop(a, r).wait_send()
-            red_down(a, r).wait_send()
-        for i in range(ring):
-            side(i, r).wait_send()
-        swap(r).wait_send()
-
-
-def over_batch(fetched, basis_values, weights, batch_count):
+    def drain():
+        for r in range(regions):
+            for a in range(far):
+                up_hop(a, r).wait_send()
+                red_up(a, r).wait_send()
+            for a in range(near):
+                down_hop(a, r).wait_send()
+                red_down(a, r).wait_send()
+            for i in range(ring):
+                side(i, r).wait_send()
+            swap(r).wait_send()
+
+    return drain
+
+
+def batch_scratch(basis_values, requests, rows, batch_count):
     ring = batch_count // 2
     far = ring // 2
     near = ring - 1 - far
-    regions = basis_values.shape[0]
-    requests, rows, width = fetched.shape
+    regions, _, _, width = basis_values.shape
     dma = pltpu.SemaphoreType.DMA
     half = jnp.bfloat16
-    vmem = pl.BlockSpec(memory_space=pltpu.VMEM)
-    return pl.pallas_call(
-        functools.partial(batch_kernel, ring, far, regions, rows),
-        out_shape=jax.ShapeDtypeStruct((requests, rows, width), half),
-        in_specs=[vmem, pl.BlockSpec(memory_space=pltpu.HBM), vmem],
-        out_specs=vmem,
-        scratch_shapes=[
-            pltpu.VMEM(basis_values.shape, half), dma((regions,)),
-            pltpu.VMEM((requests, batch_count, rows, width), half),
-            pltpu.VMEM((requests, ring, 2, rows, width), half),
-            pltpu.VMEM((requests, ring, rows, width), half),
-            pltpu.VMEM((far, requests, rows, width), half),
-            pltpu.VMEM((far, requests, rows, width), half),
-            pltpu.VMEM((near, requests, rows, width), half),
-            pltpu.VMEM((near, requests, rows, width), half),
-            dma((far, regions)), dma((far, regions)),
-            dma((near, regions)), dma((near, regions)),
-            dma((ring, regions)), dma((ring, regions)),
-            dma((regions,)), dma((regions,)),
-            dma((far, regions)), dma((far, regions)),
-            dma((near, regions)), dma((near, regions)),
-        ],
-        compiler_params=pltpu.CompilerParams(
-            collective_id=0, has_side_effects=True, vmem_limit_bytes=48 * 1024 * 1024
-        ),
-        name="over_batch",
-    )(fetched, basis_values, weights)
+    return [
+        pltpu.VMEM(basis_values.shape, half), dma((regions,)),
+        pltpu.VMEM((requests, batch_count, rows, width), half),
+        pltpu.VMEM((requests, ring, 2, rows, width), half),
+        pltpu.VMEM((requests, ring, rows, width), half),
+        pltpu.VMEM((far, requests, rows, width), half),
+        pltpu.VMEM((far, requests, rows, width), half),
+        pltpu.VMEM((near, requests, rows, width), half),
+        pltpu.VMEM((near, requests, rows, width), half),
+        dma((far, regions)), dma((far, regions)),
+        dma((near, regions)), dma((near, regions)),
+        dma((ring, regions)), dma((ring, regions)),
+        dma((regions,)), dma((regions,)),
+        dma((far, regions)), dma((far, regions)),
+        dma((near, regions)), dma((near, regions)),
+    ]
 
 
 def plane(columns, ring):
@@ -264,14 +250,7 @@
     def along_x(d):
         return lax.rem(x + d, columns) * ring + z
 
-    def greet():
-        barrier = pltpu.get_barrier_semaphore()
-        targets = [along_z(1), along_z(-1)] + [along_x(d) for d in range(1, columns)]
-        for target in targets:
-            pl.semaphore_signal(barrier, inc=1, device_id={"region": target}, device_id_type=MESH)
-        pl.semaphore_wait(barrier, len(targets))
-
-    return m, x, z, at, along_z, along_x, greet
+    return x, at, along_z, along_x
 
 
 def to_region(src, dst, send, recv, target):
@@ -285,9 +264,7 @@
                  up_send, up_recv, down_send, down_recv, x_send, x_recv, *held):
     near = ring - 1 - far
     kept = own_ref.shape[0]
-    m, x, z, at, along_z, along_x, greet = plane(columns, ring)
-    greet()
-
+    x, at, along_z, along_x = plane(columns, ring)
     def source(i):
         return own_ref if i == 0 else held[i - 1]
 
@@ -342,14 +319,18 @@
             arrival(d, i).wait_recv()
     for j in range(out_ref.shape[0]):
         out_ref[j] = landed[owner_ref[j]]
-    for t in range(kept):
-        for a in range(far):
-            up(a, t).wait_send()
-        for a in range(near):
-            down(a, t).wait_send()
-    for i in range(ring):
-        for d in range(1, columns):
-            across(d, i).wait_send()
+
+    def drain():
+        for t in range(kept):
+            for a in range(far):
+                up(a, t).wait_send()
+            for a in range(near):
+                down(a, t).wait_send()
+        for i in range(ring):
+            for d in range(1, columns):
+                across(d, i).wait_send()
+
+    return drain
 
 
 def give_kernel(columns, ring, far, table_ref, request_ref, pairs_ref, out_ref, stage, landed,
@@ -357,9 +338,7 @@
                 up_send, up_recv, down_send, down_recv, x_send, x_recv):
     near = ring - 1 - far
     kept = out_ref.shape[0]
-    m, x, z, at, along_z, along_x, greet = plane(columns, ring)
-    greet()
-
+    x, at, along_z, along_x = plane(columns, ring)
     def across(d, i):
         return to_region(
             stage.at[d - 1, i], landed.at[d - 1, i], x_send.at[d - 1, i], x_recv.at[d - 1, i], along_x(d)
@@ -436,21 +415,6 @@
             across(d, k % ring).wait_send()
 
 
-def over_region(kernel, name, collective_id, scratch, out, columns, ring, far, table, index, values):
-    vmem, smem = pl.BlockSpec(memory_space=pltpu.VMEM), pl.BlockSpec(memory_space=pltpu.SMEM)
-    return pl.pallas_call(
-        functools.partial(kernel, columns, ring, far),
-        out_shape=out,
-        in_specs=[smem, smem, vmem],
-        out_specs=vmem,
-        scratch_shapes=scratch,
-        compiler_params=pltpu.CompilerParams(
-            collective_id=collective_id, has_side_effects=True, vmem_limit_bytes=32 * 1024 * 1024
-        ),
-        name=name,
-    )(table, index, values)
-
-
 COLUMNS = 4
 
 
@@ -463,35 +427,68 @@
     ]
 
 
-def fetch(table, my_owners, dens_tiles, ring):
-    far = ring // 2
-    kept, rows, width = dens_tiles.shape
-    kind = dens_tiles.dtype
+def fetch_scratch(ring, kept, rows, width, kind):
     scratch = [
         pltpu.VMEM((COLUMNS - 1, ring, rows, width), kind),
         pltpu.VMEM((COLUMNS * ring, rows, width), kind),
     ]
-    scratch += plane_semaphores(COLUMNS, ring, far, kept)
-    scratch += [pltpu.VMEM((kept, rows, width), kind)] * (ring - 1)
-    out = jax.ShapeDtypeStruct((my_owners.shape[0], rows, width), kind)
-    return over_region(
-        fetch_kernel, "fetch", 1, scratch, out, COLUMNS, ring, far, table, my_owners, dens_tiles
-    )
-
-
-def give(table, request, pairs, kept, ring):
+    scratch += plane_semaphores(COLUMNS, ring, ring // 2, kept)
+    return scratch + [pltpu.VMEM((kept, rows, width), kind)] * (ring - 1)
+
+
+def give_scratch(ring, kept, rows, width, kind):
     far = ring // 2
     near = ring - 1 - far
-    rows, width = pairs.shape[1:]
-    kind = pairs.dtype
     scratch = [pltpu.VMEM((COLUMNS - 1, ring, rows, width), kind)] * 2
     scratch += [pltpu.VMEM((far, kept, rows, width), kind)] * 2
     scratch += [pltpu.VMEM((near, kept, rows, width), kind)] * 2
-    scratch += plane_semaphores(COLUMNS, ring, far, kept)
-    out = jax.ShapeDtypeStruct((kept, rows, width), jnp.float32)
-    return over_region(
-        give_kernel, "give", 2, scratch, out, COLUMNS, ring, far, table, request, pairs
-    )
+    return scratch + plane_semaphores(COLUMNS, ring, far, kept)
+
+
+def whole_kernel(ring, y_ring, regions, rows, counts, table_ref, owner_ref, request_ref, dens_ref,
+                 basis_ref, weight_ref, out_ref, fetched, pairs, *scratch):
+    x, at, along_z, along_x = plane(COLUMNS, ring)
+    me = lax.axis_index("batch")
+    barrier = pltpu.get_barrier_semaphore()
+    targets = [{"region": along_z(1)}, {"region": along_z(-1)}]
+    targets += [{"region": along_x(d)} for d in range(1, COLUMNS)]
+    targets += [{"batch": lax.rem(me + k, 2 * y_ring)} for k in (2, 2 * y_ring - 2)]
+    targets += [{"batch": me // 2 * 2 + 1 - me % 2}]
+    for target in targets:
+        pl.semaphore_signal(barrier, inc=1, device_id=target, device_id_type=MESH)
+    pl.semaphore_wait(barrier, len(targets))
+    first, second = counts
+    drains = [
+        fetch_kernel(COLUMNS, ring, ring // 2, table_ref, owner_ref, dens_ref, fetched, *scratch[:first]),
+        batch_kernel(y_ring, y_ring // 2, regions, rows, fetched, basis_ref, weight_ref, pairs,
+                     *scratch[first:second]),
+    ]
+    give_kernel(COLUMNS, ring, ring // 2, table_ref, request_ref, pairs, out_ref, *scratch[second:])
+    for drain in drains:
+        drain()
+
+
+def exchange(table, my_owners, request, dens_tiles, basis_values, weights, ring, batch_count):
+    kept, rows, width = dens_tiles.shape
+    kind = dens_tiles.dtype
+    requests = my_owners.shape[0]
+    regions = basis_values.shape[0]
+    first = fetch_scratch(ring, kept, rows, width, kind)
+    second = batch_scratch(basis_values, requests, rows, batch_count)
+    third = give_scratch(ring, kept, rows, width, kind)
+    counts = (len(first), len(first) + len(second))
+    vmem, smem = pl.BlockSpec(memory_space=pltpu.VMEM), pl.BlockSpec(memory_space=pltpu.SMEM)
+    return pl.pallas_call(
+        functools.partial(whole_kernel, ring, batch_count // 2, regions, rows, counts),
+        out_shape=jax.ShapeDtypeStruct((kept, rows, width), jnp.float32),
+        in_specs=[smem, smem, smem, vmem, pl.BlockSpec(memory_space=pltpu.HBM), vmem],
+        out_specs=vmem,
+        scratch_shapes=[pltpu.VMEM((requests, rows, width), kind)] * 2 + first + second + third,
+        compiler_params=pltpu.CompilerParams(
+            collective_id=0, has_side_effects=True, vmem_limit_bytes=52 * 1024 * 1024
+        ),
+        name="exchange",
+    )(table, my_owners, request, dens_tiles, basis_values, weights)
 
 
 def shards(basis_values, dens_tiles, region_tiles, point_counts, point_weights):
@@ -515,11 +512,11 @@
     table = wanted.reshape(COLUMNS, ring, COLUMNS, ring)
     table = lax.dynamic_index_in_dim(table, my_index % ring, 1, keepdims=False)
     table = lax.dynamic_index_in_dim(table, my_index // ring, 1, keepdims=False)
-    fetched = fetch(table, my_owners, dens_tiles, ring)
     live = jnp.arange(point_local, dtype=jnp.int32)[None, :] < point_counts
     weights = jnp.where(live, point_weights, 0.0)[:, :, None]
-    pairs = over_batch(fetched, basis_values, weights, batch_count)
-    return give(table, request, pairs, tile_local, ring)
+    return exchange(
+        table, my_owners, request, dens_tiles, basis_values, weights, ring, batch_count
+    )
 
 
 def solution(mesh):

time: 138 us -> 130 us (0.942)
  Pallas kernels: 132 us -> 126 us
  local copies, waits for them, and re-layouts: 4.77 us -> 3.18 us
    pallas_call x3 -> x1, Pallas kernels: 132 us -> 126 us  [exchange(): pl.pallas_call(functools.partial(whole_kernel, ring, batch_count // 2, re...]
    unnamed x6 -> x4, local copies, waits for them, and re-layouts: 3.98 us -> 2.4 us
where the time goes in v5:
time: 130 us
  Pallas kernels  126 us (97%)
  local copies, waits for them, and re-layouts  3.18 us (2%)
    pallas_call x1, Pallas kernels, exchange(): pl.pallas_call(functools.partial(whole_kernel, ring, batch_count // 2, re...  126 us

profile of v5, /device:TPU:4, one launch (start us, length us, event | category | flops | bytes accessed | tf_op | source)
XLA Modules:
  0.0 129.9 jit_solution(755220003945273087)
XLA Ops:
  0.0 0.8 select_bitcast_fusion
  0.8 0.8 copy.18
  1.5 0.1 reshape.65
  1.6 0.1 copy.19
  1.7 0.2 dynamic-slice_reduce_fusion.owner_ref
  1.9 0.2 select_reduce_fusion
  2.1 0.1 reshape.66.request_ref
  2.2 0.1 sub.18
  2.3 0.2 copy.23.weight_ref
  2.6 0.0 copy-start
  2.6 0.9 copy-done
  3.5 125.7 %exchange.1 = f32[4,32,512]{2,1,0:T(8,128)S(1)} custom-call(s32[4,8]{1,0:T(4,128)S(1)} %bitcast.4, s32[12]{0:T(128)S(1)} %dynamic-slice_reduce_fusion.owner_ref, s32[4,8]{1,0:T(4,128)S(1)} %reshape.66.request_ref, bf16[4,32,512]{2,1,0:T(8,128)(2,1)S(1)} %copy-done, bf16[4,2,256,512]{3,2,1,0:T(8,128)(2,1)} %basis_ref.1, f32[4,256,1]{2,1,0:T(8,128)S(1)} %copy.23.weight_ref), custom_call_target="tpu_custom_call" | custom-call | tf_op jit(solution)/shard_map/exchange/pallas_call | solution.py:481
  129.1 0.7 copy.25
  (4 shorter events, 0.1 us)
Async XLA Ops:
  2.6 0.9 copy-start
